TPU v7x, 256 devices: a whole 4x4x8 slice. The times are simulated.
256 devices in a mesh: dp: 16 (over x_lo, z), expert: 16 (over y, x_hi, core).
Axes of the slice: x: 4 (x_hi: 2, x_lo: 2; x = x_hi * 2 + x_lo), y: 4, z: 8, core: 2. Of those that a mesh axis runs over, the one named last changes fastest.
Arguments:
- out_grad: bfloat16 [32768, 4096], P(('dp', 'expert')), may hold values from -6 to 6
- expert_ids: int32 [32768, 4], P(('dp', 'expert')), may hold values from 0 to 15, all different within a row; in each aligned block of 128 rows (0 to 127, 128 to 255, ...) at most 48 rows name the same one
- gate_weights: bfloat16 [32768, 4], P(('dp', 'expert')), may hold values from 0.019897461 to 0.5
- saved_acts: bfloat16 [16, 16, 16, 48, 1536], P('dp', None, 'expert'), may hold values from -8 to 8
- down_weight: bfloat16 [16, 4096, 768], P('expert', 'dp'), may hold values from -0.09375 to 0.09375
Outputs:
- pre_grads: bfloat16 [16, 16, 16, 48, 1536], P('dp', None, 'expert')
- down_grad: bfloat16 [16, 4096, 768], P('expert', 'dp')
- gate_grad: float32 [32768, 4], P(('dp', 'expert'))
Inputs may be any that keep to these rules, and one draw needn't show every extreme that they name: `expert_ids`: each token names 4 different experts; among the 128 tokens of one device no expert is named by more than 48 tokens, a bound that some block reaches.
All inputs are finite; a program needn't handle non-finite values.
Results may differ from a plain program's by a relative error of at most 0.0057.
Values may be sent and summed in bfloat16 or wider, within the bound.
A program may use at most 192 MiB of HBM per device.

v0:
```python
import jax
import jax.numpy as jnp
from jax import lax
from jax.sharding import PartitionSpec as P

EXPERTS = 16
CAP = 48


def slot_numbers(choice_rows):
    hits = jnp.sum(
        (choice_rows[:, :, None] == jnp.arange(EXPERTS, dtype=jnp.int32)[None, None, :]).astype(
            jnp.int32
        ),
        axis=1,
    )
    before = jnp.cumsum(hits, axis=0) - hits
    return jnp.take_along_axis(before, choice_rows, axis=1)


def shards(out_grad, expert_ids, gate_weights, saved_acts, down_weight):
    sources = lax.axis_size("expert")
    local_count = down_weight.shape[0]
    hidden_width = down_weight.shape[2]
    width = out_grad.shape[1]
    tok_rows = out_grad.shape[0]
    top_count = expert_ids.shape[1]
    own_slots = slot_numbers(expert_ids)
    own_target = expert_ids * CAP + own_slots
    total_slots = sources * local_count * CAP
    flat_target = own_target.reshape(-1)
    copies = jnp.broadcast_to(out_grad[:, None, :], (tok_rows, top_count, width)).reshape(-1, width)
    outgoing = jnp.zeros((total_slots, width), jnp.bfloat16).at[flat_target].set(copies)
    outgoing = outgoing.reshape(sources, local_count, CAP, width)
    gate_out = jnp.zeros((total_slots,), jnp.bfloat16).at[flat_target].set(gate_weights.reshape(-1))
    gate_out = gate_out.reshape(sources, local_count, CAP)
    routed, gate_slot = (
        lax.all_to_all(outgoing, "expert", split_axis=0, concat_axis=0, tiled=True),
        lax.all_to_all(gate_out, "expert", split_axis=0, concat_axis=0, tiled=True),
    )
    saved = saved_acts[0]
    gate_pre = saved[..., :hidden_width].astype(jnp.float32)
    up_pre = saved[..., hidden_width:].astype(jnp.float32)
    sigma = jax.nn.sigmoid(gate_pre)
    silu_val = gate_pre * sigma
    act = silu_val * up_pre
    act_low = act.astype(jnp.bfloat16)
    back = jnp.einsum(
        "slcd,ldf->slcf",
        routed,
        lax.all_gather(down_weight, "dp", axis=1, tiled=True),
        preferred_element_type=jnp.float32,
    )
    score = jnp.sum(back * act, axis=3)
    gate_f = gate_slot.astype(jnp.float32)[..., None]
    grad_act = gate_f * back
    d_gate = grad_act * up_pre * sigma * (1.0 + gate_pre * (1.0 - sigma))
    d_up = grad_act * silu_val
    pre_grads = jnp.concatenate([d_gate, d_up], axis=3).astype(jnp.bfloat16)[None]
    weighted = (gate_f * routed.astype(jnp.float32)).astype(jnp.bfloat16)
    summed = lax.psum_scatter(
        jnp.einsum("slcd,slcf->dlf", weighted, act_low, preferred_element_type=jnp.float32),
        "dp",
        scatter_dimension=0,
        tiled=True,
    )
    down_grad = jnp.transpose(summed, (1, 0, 2)).astype(jnp.bfloat16)
    returned = lax.all_to_all(score, "expert", split_axis=0, concat_axis=0, tiled=True)
    gate_grad = jnp.take(returned.reshape(-1), own_target.reshape(-1)).reshape(tok_rows, top_count)
    return (pre_grads, down_grad, gate_grad)


def solution(mesh):
    placed = (
        P(("dp", "expert"), None),
        P(("dp", "expert"), None),
        P(("dp", "expert"), None),
        P("dp", None, "expert", None, None),
        P("expert", "dp", None),
    )
    return jax.shard_map(
        shards,
        mesh=mesh,
        in_specs=placed,
        out_specs=(
            P("dp", None, "expert", None, None),
            P("expert", "dp", None),
            P(("dp", "expert"), None),
        ),
        check_vma=False,
    )
```

profile of v0, /device:TPU:1, one launch (start us, length us, event | category | flops | bytes accessed | tf_op | source)
XLA Modules:
  0.0 322.6 jit_solution(18109848822992749731)
XLA Ops:
  7.2 0.7 all-gather.2.cloned.1.call-update
  7.9 0.8 copy.67
  8.7 0.1 reshape.175
  8.8 0.7 convert_reduce_fusion
  9.6 0.7 bitcast_or_fusion
  10.3 0.1 copy.64
  10.4 0.1 reshape.165
  10.5 0.2 reduce_window_sum.11
  10.7 3.8 %gather_fusion.1 = s32[512]{0:T(512)S(1)} fusion(s32[128,16]{1,0:T(8,128)S(1)} %sub.6, s32[512]{0:T(512)S(1)} %reshape.165), kind=kCustom, calls=%fused_computation.1 | custom fusion | bytes 8192 | tf_op jit(solution)/shard_map/jit(take_along_axis)/gather | solution.py:18
  14.7 0.1 copy.66
  14.8 0.1 reshape.146
  15.0 3.8 %scatter_custom_fusion = bf16[768]{0:T(1024)(128)(2,1)S(1)} fusion(s32[512]{0:T(512)S(1)} %bitcast.59, bf16[512]{0:T(512)(128)(2,1)S(1)} %reshape.175, bf16[]{:T(256)} %constant.15.clone.1), kind=kCustom, calls=%fused_computation.45 | custom fusion | bytes 1538 | tf_op jit(solution)/shard_map/scatter | solution.py:35
  18.7 0.7 reshape.194
  19.4 8.4 %all-to-all-start = ((bf16[16,1,48]{2,1,0:T(2,128)(2,1)}), bf16[16,1,48]{2,1,0:T(2,128)(2,1)S(1)}, u32[]{:S(2)}, u32[]{:S(2)}) async-start(bf16[16,1,48]{2,1,0:T(2,128)(2,1)} %reshape.194), calls=%async_computation | async-start | bytes 16384 | tf_op jit(solution)/shard_map/all_to_all | solution.py:39
  27.9 4.0 %broadcast_in_dim.31 = bf16[128,4,4096]{2,1,0:T(4,128)(2,1)} broadcast(bf16[128,4096]{1,0:T(8,128)(2,1)S(1)} %copy-done), dimensions={0,2} | broadcast | bytes 5242880 | tf_op jit(solution)/shard_map/broadcast_in_dim | solution.py:32
  31.9 7.0 %reshape.183 = bf16[512,4096]{1,0:T(8,128)(2,1)} reshape(bf16[128,4,4096]{2,1,0:T(4,128)(2,1)} %broadcast_in_dim.31) | data formatting | bytes 8388608 | tf_op jit(solution)/shard_map/reshape | solution.py:32
  38.9 11.4 %scatter_custom_fusion.1 = bf16[768,4096]{1,0:T(8,128)(2,1)} fusion(s32[512]{0:T(512)S(1)} %bitcast.60, bf16[512,4096]{1,0:T(8,128)(2,1)} %reshape.183, bf16[]{:T(256)} %constant.15.clone.1), kind=kCustom, calls=%fused_computation.14 | custom fusion | bytes 6291968 | tf_op jit(solution)/shard_map/scatter | solution.py:33
  50.3 7.2 %all-to-all-start.1 = ((bf16[16,1,48,4096]{3,2,1,0:T(8,128)(2,1)}), bf16[16,1,48,4096]{3,2,1,0:T(8,128)(2,1)}, u32[]{:S(2)}, u32[]{:S(2)}) async-start(bf16[16,1,48,4096]{3,2,1,0:T(8,128)(2,1)} %bitcast.58), calls=%async_computation.1 | async-start | bytes 12582912 | tf_op jit(solution)/shard_map/all_to_all | solution.py:38
  57.5 0.3 reduce-scatter.2.cloned.1.call-start
  57.8 106.5 %all-to-all-done.1 = bf16[16,1,48,4096]{3,2,1,0:T(8,128)(2,1)} async-done(((bf16[16,1,48,4096]{3,2,1,0:T(8,128)(2,1)}), bf16[16,1,48,4096]{3,2,1,0:T(8,128)(2,1)}, u32[]{:S(2)}, u32[]{:S(2)}) %all-to-all-start.1) | async-done | bytes 6291488 | tf_op jit(solution)/shard_map/all_to_all | solution.py:38
  164.3 11.3 %convolution_bitcast_fusion = f32[4096,1,768]{0,2,1:T(8,128)} fusion(bf16[16,1,48,4096]{3,2,1,0:T(8,128)(2,1)} %all-to-all-done.1, f32[16,48]{1,0:T(8,128)S(1)} %bitcast.62, bf16[16,1,48,1536]{3,2,0,1:T(8,128)(2,1)} %bitcast.64), kind=kOutput, calls=%fused_computation.5 | convolution fusion | flops 4845993984 | bytes 21236736 | tf_op jit(solution)/shard_map/slcd,slcf->dlf/dot_general | solution.py:62
  175.7 11.0 %fusion.20 = (bf16[1,16,1,48,768]{4,3,1,2,0:T(8,128)(2,1)S(1)}, bf16[1,16,1,48,768]{4,3,1,2,0:T(8,128)(2,1)S(1)}, f32[16,48]{1,0:T(8,128)}) fusion(f32[16,48]{1,0:T(8,128)S(1)} %bitcast.63, bf16[16,1,48,1536]{3,2,0,1:T(8,128)(2,1)} %bitcast.65, bf16[1,4096,768]{2,1,0:T(8,128)(2,1)} %all-gather.2.cloned.1.call-done, bf16[16,1,48,4096]{3,2,1,0:T(8,128)(2,1)} %all-to-all-done.1), kind=kOutput, calls=%fused_computation.33 | convolution fusion | flops 4843043840 | bytes 17307648 | tf_op jit(solution)/shard_map/slcd,ldf->slcf/dot_general | solution.py:48
  186.7 3.7 %all-to-all-start.2 = ((f32[16,1,48]{2,1,0:T(1,128)}), f32[16,1,48]{2,1,0:T(1,128)S(1)}, u32[]{:S(2)}, u32[]{:S(2)}) async-start(f32[16,1,48]{2,1,0:T(1,128)} %bitcast.22), calls=%async_computation.3 | async-start | bytes 16384 | tf_op jit(solution)/shard_map/all_to_all | solution.py:68
  190.4 1.6 maximum_bitcast_fusion
  192.0 5.5 %all-to-all-done.2 = f32[16,1,48]{2,1,0:T(1,128)S(1)} async-done(((f32[16,1,48]{2,1,0:T(1,128)}), f32[16,1,48]{2,1,0:T(1,128)S(1)}, u32[]{:S(2)}, u32[]{:S(2)}) %all-to-all-start.2) | async-done | bytes 3104 | tf_op jit(solution)/shard_map/all_to_all | solution.py:68
  197.6 0.5 broadcast.93
  198.1 0.7 reduce.4
  198.8 2.3 gather_fusion
  201.3 0.6 and_select_fusion
  201.9 111.8 %reduce-scatter.2.cloned.1.call-done = f32[256,1,768]{0,2,1:T(8,128)} async-done(((f32[4096,1,768]{0,2,1:T(8,128)}), f32[256,1,768]{0,2,1:T(8,128)}) %reduce-scatter.2.cloned.1.call-update) | async-done | bytes 786448 | tf_op jit(solution)/shard_map/reduce_scatter | solution.py:61
  313.7 1.2 convert_bitcast_fusion
  314.9 0.9 copy.71
  (19 shorter events, 0.6 us)
Async XLA Ops:
  7.2 168.5 %all-gather.2.cloned.1.call-start = ((), (), s32[]{:S(2)}) async-start(), calls=%async_computation.4 | async-start | bytes 6684672 | tf_op jit(solution)/shard_map/all_gather | solution.py:51
  10.7 4.0 %copy-start.1 = (s32[128,4]{0,1:T(4,128)S(1)}, s32[128,4]{0,1:T(4,128)}, u32[]{:S(2)}) copy-start(s32[128,4]{0,1:T(4,128)} %param.6) | copy-start | bytes 6148
  10.7 17.1 %copy-start = (bf16[128,4096]{1,0:T(8,128)(2,1)S(1)}, bf16[128,4096]{1,0:T(8,128)(2,1)}, u32[]{:S(2)}) copy-start(bf16[128,4096]{1,0:T(8,128)(2,1)} %param.5) | copy-start | bytes 3145732
  19.4 30.9 %all-to-all-start = ((bf16[16,1,48]{2,1,0:T(2,128)(2,1)}), bf16[16,1,48]{2,1,0:T(2,128)(2,1)S(1)}, u32[]{:S(2)}, u32[]{:S(2)}) async-start(bf16[16,1,48]{2,1,0:T(2,128)(2,1)} %reshape.194), calls=%async_computation | async-start | bytes 16384 | tf_op jit(solution)/shard_map/all_to_all | solution.py:39
  50.3 114.0 %all-to-all-start.1 = ((bf16[16,1,48,4096]{3,2,1,0:T(8,128)(2,1)}), bf16[16,1,48,4096]{3,2,1,0:T(8,128)(2,1)}, u32[]{:S(2)}, u32[]{:S(2)}) async-start(bf16[16,1,48,4096]{3,2,1,0:T(8,128)(2,1)} %bitcast.58), calls=%async_computation.1 | async-start | bytes 12582912 | tf_op jit(solution)/shard_map/all_to_all | solution.py:38
  57.5 256.2 %reduce-scatter.2.cloned.1.call-start = ((), (), s32[]{:S(2)}) async-start(), calls=%async_computation.5 | async-start | bytes 13369344 | tf_op jit(solution)/shard_map/reduce_scatter | solution.py:61
  186.7 10.8 %all-to-all-start.2 = ((f32[16,1,48]{2,1,0:T(1,128)}), f32[16,1,48]{2,1,0:T(1,128)S(1)}, u32[]{:S(2)}, u32[]{:S(2)}) async-start(f32[16,1,48]{2,1,0:T(1,128)} %bitcast.22), calls=%async_computation.3 | async-start | bytes 16384 | tf_op jit(solution)/shard_map/all_to_all | solution.py:68
Sparse Core Ops, SparseCore 0:
  9.8 82.2 all-gather.1
  175.8 137.8 reduce-scatter.1
where the time goes:
time: 323 us
  waiting for transfers between devices  225 us (70%)
  local copies, waits for them, and re-layouts  36.3 us (11%)
  matrix products  22.4 us (7%)
  starting transfers between devices  19.6 us (6%)
  between operations  14.2 us (4%)
  other arithmetic  5.69 us (2%)
    reduce_scatter x1, waiting for transfers between devices, shards(): lax.psum_scatter(jnp.einsum('slcd,slcf->dlf', weighted, act_low, preferre...  112 us
    all_to_all x1, waiting for transfers between devices, shards(): lax.all_to_all(outgoing, 'expert', split_axis=0, concat_axis=0, tiled=True)  106 us
    scatter x1, local copies, waits for them, and re-layouts, shards(): jnp.zeros((total_slots, width), jnp.bfloat16).at[flat_target].set(copies)  11.4 us
    dot_general x1, matrix products, shards(): jnp.einsum('slcd,slcf->dlf', weighted, act_low, preferred_element_type=jn...  11.3 us
    dot_general x1, matrix products, shards(): jnp.einsum('slcd,ldf->slcf', routed, lax.all_gather(down_weight, 'dp', ax...  11 us
    all_to_all x1, starting transfers between devices, shards(): lax.all_to_all(gate_out, 'expert', split_axis=0, concat_axis=0, tiled=True)  8.45 us
    all_to_all x1, starting transfers between devices, shards(): lax.all_to_all(outgoing, 'expert', split_axis=0, concat_axis=0, tiled=True)  7.18 us
    reshape x1, local copies, waits for them, and re-layouts, shards(): jnp.broadcast_to(out_grad[:, None, :], (tok_rows, top_count, width))  6.96 us
  transfers between devices with their start and end apart: 5, of which 3 were waited for; matrix products, arithmetic and copies ran while one was open for 19% of the time, Pallas kernels for 0%

commit v1 on v0

v1 whole, which is shorter than its diff:
```python
import jax
import jax.numpy as jnp
from jax import lax
from jax.experimental import pallas as pl
from jax.experimental.pallas import tpu as pltpu
from jax.sharding import PartitionSpec as P

MESH = pl.DeviceIdType.MESH
F32 = jnp.float32
BF16 = jnp.bfloat16

EXPERTS = 16
CAP = 48
TOK = 128
FF = 768
DZ = 256
NQ = 8
NZ = 8
NY = 4
DELTA = (4, 3, -3, 2, -2, 1, -1, 0)


def kernel(
    og_ref, ids_ref, saved_ref, w_ref,
    pre_ref, down_ref, gate_ref,
    tok, routed, stage, sel, gate, meta, wall, act_low, fac_g, fac_u, acc,
    rs_half, rs_out, rs_half_in, rs_in, fin_out, fin_in, own_sum, sc_out, sc_in,
    a_send, a_recv, s_send, s_recv, m_send, m_recv,
    bz_send, bz_recv, bx_send, bx_recv, c_send, c_recv, f_send, f_recv, g_send, g_recv,
):
    dp = lax.axis_index("dp")
    ex = lax.axis_index("expert")
    xl, z = dp // NZ, lax.rem(dp, NZ)
    y, xh, core = ex // 4, lax.rem(ex // 2, 2), lax.rem(ex, 2)

    def around_z(d):
        return lax.rem(z + (d + NZ), NZ)

    def around_y(d):
        return lax.rem(y + (d + NY), NY)

    def at_z(d):
        return {"dp": xl * NZ + around_z(d)}

    def at_y(d):
        return {"expert": (around_y(d) * 2 + xh) * 2 + core}

    x_mate = {"dp": (1 - xl) * NZ + z}
    h_mate = {"expert": (y * 2 + (1 - xh)) * 2 + core}
    c_mate = {"expert": (y * 2 + xh) * 2 + (1 - core)}

    def remote(src, dst, send, recv, to):
        return pltpu.make_async_remote_copy(
            src_ref=src, dst_ref=dst, send_sem=send, recv_sem=recv, device_id=to, device_id_type=MESH
        )

    barrier = pltpu.get_barrier_semaphore()

    def greet(i, carry):
        pl.semaphore_signal(
            barrier, inc=1, device_id={"expert": lax.rem(ex + i, EXPERTS)}, device_id_type=MESH
        )
        return carry

    lax.fori_loop(1, EXPERTS, greet, 0)
    for to in (x_mate, at_z(1), at_z(-1)):
        pl.semaphore_signal(barrier, inc=1, device_id=to, device_id_type=MESH)
    pl.semaphore_wait(barrier, EXPERTS + 2)

    me8 = y * 2 + xh
    ym8, yp8 = around_y(-1) * 2 + xh, around_y(1) * 2 + xh
    y2 = around_y(2) * 2 + xh
    flip = 1 - 2 * xh
    lower, upper = pl.ds(0, TOK // 2), pl.ds(TOK // 2, TOK // 2)

    def a_copy(kind, q, src8, rows, to):
        ref = tok.at[src8, q] if rows is None else tok.at[src8, q, rows]
        return remote(ref, ref, a_send.at[kind, q], a_recv.at[kind, q], to)

    def a_out(kind, q):
        return (
            lambda: a_copy(0, q, me8, None, h_mate),
            lambda: a_copy(1, q, me8, None, at_y(1)),
            lambda: a_copy(2, q, me8, None, at_y(-1)),
            lambda: a_copy(3, q, me8 + flip, None, at_y(1)),
            lambda: a_copy(4, q, me8 + flip, None, at_y(-1)),
            lambda: a_copy(5, q, ym8, lower, at_y(1)),
            lambda: a_copy(6, q, yp8, upper, at_y(-1)),
            lambda: a_copy(7, q, ym8 + flip, lower, at_y(1)),
            lambda: a_copy(8, q, yp8 + flip, upper, at_y(-1)),
        )[kind]()

    def a_in(kind, q):
        return (
            lambda: a_copy(0, q, me8 + flip, None, h_mate),
            lambda: a_copy(1, q, ym8, None, at_y(1)),
            lambda: a_copy(2, q, yp8, None, at_y(-1)),
            lambda: a_copy(3, q, ym8 + flip, None, at_y(1)),
            lambda: a_copy(4, q, yp8 + flip, None, at_y(-1)),
            lambda: a_copy(5, q, y2, lower, at_y(1)),
            lambda: a_copy(6, q, y2, upper, at_y(-1)),
            lambda: a_copy(7, q, y2 + flip, lower, at_y(1)),
            lambda: a_copy(8, q, y2 + flip, upper, at_y(-1)),
        )[kind]()

    def a_own(q):
        zq = around_z(DELTA[q])
        for col in range(2):
            tok[me8, q, :, col * DZ : (col + 1) * DZ] = og_ref[
                :, pl.ds(pl.multiple_of(col * NZ * DZ + zq * DZ, DZ), DZ)
            ]
        for kind in (0, 1, 2):
            a_out(kind, q).start()

    half = DZ // 2

    def bz_copy(way, step, to_send):
        sign = 1 if way == 0 else -1
        dist = step - 1 if to_send else step
        ref = wall.at[around_z(-sign * dist), xl]
        if step == 4:
            ref = ref.at[pl.ds(way * half, half)]
        return remote(ref, ref, bz_send.at[way, step - 1], bz_recv.at[way, step - 1], at_z(sign))

    def bx_copy(i, mine):
        ref = wall.at[around_z(i), xl if mine else 1 - xl]
        return remote(ref, ref, bx_send.at[i], bx_recv.at[i], x_mate)

    a_own(0)
    expert_row = lax.broadcasted_iota(jnp.int32, (EXPERTS, TOK), 0).astype(F32)
    hits = jnp.zeros((EXPERTS, TOK), F32)
    gates = jnp.zeros((EXPERTS, TOK), F32)
    for k in range(4):
        eq = expert_row == ids_ref[k : k + 1, :]
        hits = hits + jnp.where(eq, 1.0, 0.0)
        gates = gates + jnp.where(eq, ids_ref[4 + k : 5 + k, :], 0.0)
    earlier = (
        lax.broadcasted_iota(jnp.int32, (TOK, TOK), 0) < lax.broadcasted_iota(jnp.int32, (TOK, TOK), 1)
    )
    before = jnp.dot(
        hits.astype(BF16), jnp.where(earlier, 1.0, 0.0).astype(BF16), preferred_element_type=F32
    )
    meta[ex, 0:EXPERTS, :] = jnp.where(hits > 0.5, before, -1.0)
    meta[ex, EXPERTS : 2 * EXPERTS, :] = gates

    def m_copy(i, slot, to):
        return remote(meta.at[slot], meta.at[slot], m_send.at[i], m_recv.at[i], {"expert": to})

    def meta_send(i, carry):
        m_copy(i, ex, lax.rem(ex + i, EXPERTS)).start()
        return carry

    lax.fori_loop(1, EXPERTS, meta_send, 0)
    a_own(1)
    wall[z, xl] = w_ref[...]
    bz_copy(0, 1, True).start()
    bz_copy(1, 1, True).start()

    def factors(s, carry):
        row = lax.rem(s, 2) * 8 + s // 2
        for part in range(2):
            lanes = pl.ds(part * (FF // 2), FF // 2)
            g = saved_ref[s, :, part * (FF // 2) : (part + 1) * (FF // 2)].astype(F32)
            u = saved_ref[s, :, FF + part * (FF // 2) : FF + (part + 1) * (FF // 2)].astype(F32)
            sig = jax.nn.sigmoid(g)
            silu = g * sig
            act_low[row, :, lanes] = (silu * u).astype(BF16)
            fac_g[row, :, lanes] = u * sig * (1.0 + g * (1.0 - sig))
            fac_u[row, :, lanes] = silu
        return carry

    lax.fori_loop(0, 16, factors, 0)

    def meta_wait(i, carry):
        m_copy(i, lax.rem(ex - i + EXPERTS, EXPERTS), ex).wait_recv()
        return carry

    lax.fori_loop(1, EXPERTS, meta_wait, 0)
    cap_row = lax.broadcasted_iota(jnp.int32, (CAP, TOK), 0).astype(F32)

    def choose(s, carry):
        hit = cap_row == meta[s, pl.ds(ex, 1), :]
        value = jnp.where(hit, meta[s, pl.ds(EXPERTS + ex, 1), :], 0.0)
        row = lax.rem(s, 2) * 8 + s // 2
        gate[row] = jnp.broadcast_to(jnp.sum(value, axis=1, keepdims=True), (CAP, TOK))
        return carry

    lax.fori_loop(0, 16, choose, 0)

    def choose_both(s8, carry):
        s = s8 * 2 + core
        mate_ex = (y * 2 + xh) * 2 + (1 - core)
        mine = cap_row == meta[s, pl.ds(ex, 1), :]
        its = cap_row == meta[s, pl.ds(mate_ex, 1), :]
        sel[s8, 0:CAP, :] = jnp.where(mine, 1.0, 0.0).astype(BF16)
        sel[s8, CAP : 2 * CAP, :] = jnp.where(its, 1.0, 0.0).astype(BF16)
        return carry

    lax.fori_loop(0, 8, choose_both, 0)

    def s_copy(q, mine):
        c = core if mine else 1 - core
        return remote(stage.at[q], routed.at[q, c], s_send.at[q], s_recv.at[q], c_mate)

    def select(q):
        def one(s8, carry):
            got = jnp.dot(sel[s8], tok[s8, q], preferred_element_type=F32).astype(BF16)
            routed[q, core, s8] = got[0:CAP]
            stage[q, s8] = got[CAP : 2 * CAP]
            return carry

        lax.fori_loop(0, 8, one, 0)
        s_copy(q, True).start()

    def partial_sum(q, col):
        rows = routed[q, :, :, :, col * DZ : (col + 1) * DZ].reshape(16 * CAP, DZ).astype(F32)
        scale = gate[...].reshape(16 * CAP, TOK)[:, 0:1]
        weighted = (rows * scale).astype(BF16)
        return lax.dot_general(
            weighted,
            act_low[...].reshape(16 * CAP, FF),
            (((0,), (0,)), ((), ())),
            preferred_element_type=F32,
        )

    def c_half(way):
        return remote(
            rs_half.at[way], rs_half_in.at[way], c_send.at[way, 0], c_recv.at[way, 0], at_z(1 - 2 * way)
        )

    def c_full(way, hop):
        return remote(
            rs_out.at[way, hop - 1],
            rs_in.at[way, hop - 1],
            c_send.at[way, hop],
            c_recv.at[way, hop],
            at_z(1 - 2 * way),
        )

    def reduce(q):
        if q == 0:
            for col in range(2):
                part = partial_sum(q, col)
                for way in range(2):
                    rs_half[way, col] = part[way * half : (way + 1) * half].astype(BF16)
            c_half(0).start()
            c_half(1).start()
            return
        if q == 7:
            return
        way, hop = (q + 1) % 2, (q + 1) // 2
        if hop == 1:
            c_half(way).wait_recv()
        else:
            c_full(way, hop - 1).wait_recv()
        for col in range(2):
            part = partial_sum(q, col)
            if hop == 1:
                mid = slice(way * half, (way + 1) * half)
                rest = slice((1 - way) * half, (2 - way) * half)
                rs_out[way, 0, col, mid] = (part[mid] + rs_half_in[way, col].astype(F32)).astype(BF16)
                rs_out[way, 0, col, rest] = part[rest].astype(BF16)
            else:
                rs_out[way, hop - 1, col] = (part + rs_in[way, hop - 2, col].astype(F32)).astype(BF16)
        c_full(way, hop).start()

    def f_copy():
        return remote(fin_out, fin_in, f_send, f_recv, x_mate)

    for t in range(NQ + 3):
        if 0 < t and t + 1 < NQ:
            a_own(t + 1)
        if t < NQ:
            a_in(0, t).wait_recv()
            a_out(3, t).start()
            a_out(4, t).start()
            a_in(1, t).wait_recv()
            a_out(5, t).start()
            a_in(2, t).wait_recv()
            a_out(6, t).start()
        if 1 <= t <= 3:
            for way in range(2):
                bz_copy(way, t, False).wait_recv()
                bz_copy(way, t + 1, True).start()
        if t == 4:
            for way in range(2):
                bz_copy(way, 4, False).wait_recv()
        bx = {1: (0,), 2: (1,), 3: (7,), 4: (2, 6), 5: (3,), 6: (5,), 7: (4,)}.get(t, ())
        for i in bx:
            bx_copy(i, True).start()
        if 0 <= t - 1 < NQ:
            a_in(3, t - 1).wait_recv()
            a_out(7, t - 1).start()
            a_in(4, t - 1).wait_recv()
            a_out(8, t - 1).start()
        if 0 <= t - 2 < NQ:
            for kind in (5, 6, 7, 8):
                a_in(kind, t - 2).wait_recv()
            select(t - 2)
        if 0 <= t - 3 < NQ:
            s_copy(t - 3, False).wait_recv()
            reduce(t - 3)

    for i in range(NZ):
        bx_copy(i, False).wait_recv()

    def back(c):
        acc[...] = jnp.zeros_like(acc)
        for q in range(NQ):
            zq = around_z(DELTA[q])
            acc[...] += jnp.dot(
                routed[q, c].reshape(8 * CAP, 2 * DZ),
                wall[zq].reshape(2 * DZ, FF),
                preferred_element_type=F32,
            )

    def g_copy(i, src, dst, to):
        return remote(sc_out.at[src], sc_in.at[dst], g_send.at[i], g_recv.at[i], {"expert": to})

    def finish(c):
        def one(s8, carry):
            s = s8 * 2 + c
            row = c * 8 + s8
            out = acc[pl.ds(pl.multiple_of(s8 * CAP, CAP), CAP), :]
            scale = gate[row][:, 0:1]
            grad = out * scale
            silu = fac_u[row]
            u = saved_ref[s, :, FF : 2 * FF].astype(F32)
            pre_ref[s, :, 0:FF] = (grad * fac_g[row]).astype(BF16)
            pre_ref[s, :, FF : 2 * FF] = (grad * silu).astype(BF16)
            score = jnp.sum(out * (silu * u), axis=1, keepdims=True)
            sc_out[s] = jnp.broadcast_to(score, (CAP, TOK))
            return carry

        lax.fori_loop(0, 8, one, 0)

    back(0)

    c_full(0, 3).wait_recv()
    c_full(1, 3).wait_recv()

    def last(col):
        return partial_sum(7, col) + rs_in[0, 2, col].astype(F32) + rs_in[1, 2, col].astype(F32)

    for col in range(2):
        own_sum[col] = last(col)
    fin_out[...] = own_sum[1 - xl].astype(BF16)
    f_copy().start()

    finish(0)
    back(1)
    finish(1)

    def score_send(i, carry):
        to = lax.rem(ex + i, EXPERTS)
        g_copy(i, to, ex, to).start()
        return carry

    lax.fori_loop(1, EXPERTS, score_send, 0)
    sc_in[ex] = sc_out[ex]

    f_copy().wait_recv()
    down_ref[...] = (own_sum[xl] + fin_in[...].astype(F32)).astype(BF16)

    def score_wait(i, carry):
        g_copy(i, ex, lax.rem(ex - i + EXPERTS, EXPERTS), ex).wait_recv()
        return carry

    lax.fori_loop(1, EXPERTS, score_wait, 0)

    rows = [jnp.zeros((1, TOK), F32) for _ in range(4)]
    for e in range(EXPERTS):
        hit = cap_row == meta[ex, e : e + 1, :]
        value = jnp.sum(jnp.where(hit, sc_in[e], 0.0), axis=0, keepdims=True)
        for k in range(4):
            rows[k] = rows[k] + jnp.where(ids_ref[k : k + 1, :] == float(e), value, 0.0)
    for k in range(4):
        gate_ref[k : k + 1, :] = rows[k]
        gate_ref[4 + k : 5 + k, :] = rows[k]

    def drain_peers(i, carry):
        to = lax.rem(ex + i, EXPERTS)
        m_copy(i, ex, to).wait_send()
        g_copy(i, to, ex, to).wait_send()
        return carry

    lax.fori_loop(1, EXPERTS, drain_peers, 0)
    for q in range(NQ):
        for kind in range(9):
            a_out(kind, q).wait_send()
        s_copy(q, True).wait_send()
        bx_copy(q, True).wait_send()
    for way in range(2):
        for step in range(1, 5):
            bz_copy(way, step, True).wait_send()
        c_half(way).wait_send()
        for hop in range(1, 4):
            c_full(way, hop).wait_send()
    f_copy().wait_send()


def shards(out_grad, expert_ids, gate_weights, saved_acts, down_weight):
    small = jnp.concatenate([expert_ids.astype(F32), gate_weights.astype(F32)], axis=1).T
    vmem = pl.BlockSpec(memory_space=pltpu.VMEM)
    dma = pltpu.SemaphoreType.DMA
    pre, down, gate_t = pl.pallas_call(
        kernel,
        out_shape=(
            jax.ShapeDtypeStruct((EXPERTS, CAP, 2 * FF), BF16),
            jax.ShapeDtypeStruct((DZ, FF), BF16),
            jax.ShapeDtypeStruct((8, TOK), F32),
        ),
        in_specs=[vmem] * 4,
        out_specs=(vmem,) * 3,
        scratch_shapes=[
            pltpu.VMEM((8, NQ, TOK, 2 * DZ), BF16),
            pltpu.VMEM((NQ, 2, 8, CAP, 2 * DZ), BF16),
            pltpu.VMEM((NQ, 8, CAP, 2 * DZ), BF16),
            pltpu.VMEM((8, 2 * CAP, TOK), BF16),
            pltpu.VMEM((16, CAP, TOK), F32),
            pltpu.VMEM((16, 2 * EXPERTS, TOK), F32),
            pltpu.VMEM((NZ, 2, DZ, FF), BF16),
            pltpu.VMEM((16, CAP, FF), BF16),
            pltpu.VMEM((16, CAP, FF), F32),
            pltpu.VMEM((16, CAP, FF), F32),
            pltpu.VMEM((8 * CAP, FF), F32),
            pltpu.VMEM((2, 2, DZ // 2, FF), BF16),
            pltpu.VMEM((2, 3, 2, DZ, FF), BF16),
            pltpu.VMEM((2, 2, DZ // 2, FF), BF16),
            pltpu.VMEM((2, 3, 2, DZ, FF), BF16),
            pltpu.VMEM((DZ, FF), BF16),
            pltpu.VMEM((DZ, FF), BF16),
            pltpu.VMEM((2, DZ, FF), F32),
            pltpu.VMEM((16, CAP, TOK), F32),
            pltpu.VMEM((16, CAP, TOK), F32),
            dma((9, NQ)), dma((9, NQ)),
            dma((NQ,)), dma((NQ,)),
            dma((EXPERTS,)), dma((EXPERTS,)),
            dma((2, 4)), dma((2, 4)),
            dma((NZ,)), dma((NZ,)),
            dma((2, 4)), dma((2, 4)),
            dma(()), dma(()),
            dma((EXPERTS,)), dma((EXPERTS,)),
        ],
        compiler_params=pltpu.CompilerParams(
            collective_id=0, has_side_effects=True, vmem_limit_bytes=60 * 1024 * 1024
        ),
    )(out_grad, small, saved_acts[0, :, 0], down_weight[0])
    return pre[None, :, None], down[None], gate_t[:4].T


def solution(mesh):
    placed = (
        P(("dp", "expert"), None),
        P(("dp", "expert"), None),
        P(("dp", "expert"), None),
        P("dp", None, "expert", None, None),
        P("expert", "dp", None),
    )
    return jax.shard_map(
        shards,
        mesh=mesh,
        in_specs=placed,
        out_specs=(
            P("dp", None, "expert", None, None),
            P("expert", "dp", None),
            P(("dp", "expert"), None),
        ),
        check_vma=False,
    )
```

time: 323 us -> 159 us (0.49)
  waiting for transfers between devices: 225 us -> 0 us
  Pallas kernels: 0 us -> 151 us
  local copies, waits for them, and re-layouts: 36.3 us -> 5.29 us
  matrix products: 22.4 us -> 0 us
  starting transfers between devices: 19.6 us -> 0 us
  between operations: 14.2 us -> 0.64 us
  other arithmetic: 5.69 us -> 1.97 us
    pallas_call x0 -> x1, Pallas kernels: none -> 151 us  [shards(): pl.pallas_call(kernel, out_shape=(jax.ShapeDtypeStruct((EXPERTS, CAP, 2 *...]
    all_to_all x3 -> x0, waiting for transfers between devices: 112 us -> none  [the longest x1 106 us: shards(): lax.all_to_all(outgoing, 'expert', split_axis=0, concat_axis=0, tiled=True)]
    reduce_scatter x1 -> x0, waiting for transfers between devices: 112 us -> none  [shards(): lax.psum_scatter(jnp.einsum('slcd,slcf->dlf', weighted, act_low, preferre...]
    dot_general x2 -> x0, matrix products: 22.4 us -> none  [the longest x1 11.3 us: shards(): jnp.einsum('slcd,slcf->dlf', weighted, act_low, preferred_element_type=jn...]
    all_to_all x3 -> x0, starting transfers between devices: 19.3 us -> none  [the longest x1 8.45 us: shards(): lax.all_to_all(gate_out, 'expert', split_axis=0, concat_axis=0, tiled=True)]
    scatter x2 -> x0, local copies, waits for them, and re-layouts: 15.2 us -> none  [the longest x1 11.4 us: shards(): jnp.zeros((total_slots, width), jnp.bfloat16).at[flat_target].set(copies)]
    reshape x5 -> x0, local copies, waits for them, and re-layouts: 7.95 us -> none  [the longest x1 6.96 us: shards(): jnp.broadcast_to(out_grad[:, None, :], (tok_rows, top_count, width))]
    gather x8 -> x0, local copies, waits for them, and re-layouts: 6.6 us -> none  [the longest x5 4.15 us: slot_numbers(): return jnp.take_along_axis(before, choice_rows, axis=1)]
  transfers between devices with their start and end apart: 5 -> 0, of which waited for: 3 -> 0; matrix products, arithmetic and copies ran while one was open for 19% -> 0% of each run, Pallas kernels for 0% -> 0%
where the time goes in v1:
time: 159 us
  Pallas kernels  151 us (95%)
  local copies, waits for them, and re-layouts  5.29 us (3%)
  other arithmetic  1.97 us (1%)
    pallas_call x1, Pallas kernels, shards(): pl.pallas_call(kernel, out_shape=(jax.ShapeDtypeStruct((EXPERTS, CAP, 2 *...  151 us
    unnamed x4, local copies, waits for them, and re-layouts  4.03 us

profile of v1, /device:TPU:1, one launch (start us, length us, event | category | flops | bytes accessed | tf_op | source)
XLA Modules:
  0.0 158.8 jit_solution(4428570434135570896)
XLA Ops:
  0.6 0.7 convert_element_type.6
  1.3 0.7 convert_element_type.7
  2.0 0.6 maximum_bitcast_fusion.ids_ref
  2.6 150.9 %shard_map.76 = (bf16[16,48,1536]{2,1,0:T(8,128)(2,1)}, bf16[256,768]{1,0:T(8,128)(2,1)}, f32[8,128]{1,0:T(8,128)}) custom-call(bf16[128,4096]{1,0:T(8,128)(2,1)} %og_ref.1, f32[8,128]{1,0:T(8,128)} %maximum_bitcast_fusion.ids_ref, bf16[16,48,1536]{2,1,0:T(8,128)(2,1)} %bitcast.10, bf16[256,768]{1,0:T(8,128)(2,1)} %bitcast.12), custom_call_target="tpu_custom_call" | custom-call | tf_op jit(solution)/shard_map/pallas_call | solution.py:406
  153.5 1.3 slice_bitcast_fusion
  154.8 0.0 copy-start
  154.8 3.3 %copy.11 = bf16[1,16,1,48,1536]{4,3,2,1,0:T(8,128)(2,1)} copy(bf16[1,16,1,48,1536]{4,3,2,1,0:T(8,128)(2,1)} %bitcast.11) | data formatting | bytes 4718592
  158.0 0.0 copy-done
  158.0 0.7 copy.12
Async XLA Ops:
  154.8 3.3 %copy-start = (bf16[256,768]{1,0:T(8,128)(2,1)S(1)}, bf16[256,768]{1,0:T(8,128)(2,1)}, u32[]{:S(2)}) copy-start(bf16[256,768]{1,0:T(8,128)(2,1)} %get-tuple-element.7) | copy-start | bytes 1179652

commit v2 on v1

v2 whole, which is shorter than its diff:
```python
import jax
import jax.numpy as jnp
from jax import lax
from jax.experimental import pallas as pl
from jax.experimental.pallas import tpu as pltpu
from jax.sharding import PartitionSpec as P

MESH = pl.DeviceIdType.MESH
F32 = jnp.float32
BF16 = jnp.bfloat16

EXPERTS = 16
CAP = 48
TOK = 128
FF = 768
DZ = 256
NQ = 8
NZ = 8
NY = 4
PIECES = (
    ((4, 0), (4, 1)),
    ((3, 0), (-3, 0)),
    ((3, 1), (-3, 1)),
    ((2, 0), (-2, 0)),
    ((2, 1), (-2, 1)),
    ((1, 0), (-1, 0)),
    ((1, 1), (-1, 1)),
    ((0, 0), (0, 1)),
)


def kernel(
    og_ref, ids_ref, saved_hbm, w_ref,
    pre_hbm, down_ref, gate_ref,
    saved_ref, pre_ref, tok, routed, stage, sel, gate, meta_low, meta, wall, act_low, fac_g, fac_u, acc,
    rs_half, rs_out, rs_half_in, rs_in, fin_out, fin_in, part, sc_out, sc_in,
    a_send, a_recv, s_send, s_recv, m_send, m_recv,
    bz_send, bz_recv, bx_send, bx_recv, bn_send, bn_recv, c_send, c_recv, f_send, f_recv,
    g_send, g_recv, og_sem, w_sem, saved_sem, pre_sem,
):
    dp = lax.axis_index("dp")
    ex = lax.axis_index("expert")
    xl, z = dp // NZ, lax.rem(dp, NZ)
    y, xh, core = ex // 4, lax.rem(ex // 2, 2), lax.rem(ex, 2)

    def around_z(d):
        return lax.rem(z + (d + NZ), NZ)

    def around_y(d):
        return lax.rem(y + (d + NY), NY)

    def at_z(d):
        return {"dp": xl * NZ + around_z(d)}

    def at_y(d):
        return {"expert": (around_y(d) * 2 + xh) * 2 + core}

    x_mate = {"dp": (1 - xl) * NZ + z}
    h_mate = {"expert": (y * 2 + (1 - xh)) * 2 + core}
    c_mate = {"expert": (y * 2 + xh) * 2 + (1 - core)}

    def remote(src, dst, send, recv, to):
        return pltpu.make_async_remote_copy(
            src_ref=src, dst_ref=dst, send_sem=send, recv_sem=recv, device_id=to, device_id_type=MESH
        )

    barrier = pltpu.get_barrier_semaphore()

    def greet(i, carry):
        pl.semaphore_signal(
            barrier, inc=1, device_id={"expert": lax.rem(ex + i, EXPERTS)}, device_id_type=MESH
        )
        return carry

    lax.fori_loop(1, EXPERTS, greet, 0)
    for to in (x_mate, at_z(1), at_z(-1)):
        pl.semaphore_signal(barrier, inc=1, device_id=to, device_id_type=MESH)

    me8 = y * 2 + xh

    def column(order):
        return 1 - xl if order == 0 else xl

    def og_copy(q, j):
        dist, order = PIECES[q][j]
        cols = pl.ds(pl.multiple_of((column(order) * NZ + around_z(dist)) * DZ, DZ), DZ)
        return pltpu.make_async_copy(
            og_ref.at[:, cols], tok.at[me8, q, :, pl.ds(j * DZ, DZ)], og_sem.at[q, j]
        )

    w_copy = pltpu.make_async_copy(w_ref, wall.at[z, xl], w_sem)
    saved_copy = pltpu.make_async_copy(saved_hbm, saved_ref, saved_sem)
    for q in range(NQ):
        for col in range(2):
            og_copy(q, col).start()
        if q == 1:
            w_copy.start()
    saved_copy.start()
    expert_row = lax.broadcasted_iota(jnp.int32, (EXPERTS, TOK), 0).astype(F32)
    hits = jnp.zeros((EXPERTS, TOK), F32)
    gates = jnp.zeros((EXPERTS, TOK), F32)
    for k in range(4):
        eq = expert_row == ids_ref[k : k + 1, :]
        hits = hits + jnp.where(eq, 1.0, 0.0)
        gates = gates + jnp.where(eq, ids_ref[4 + k : 5 + k, :], 0.0)
    earlier = (
        lax.broadcasted_iota(jnp.int32, (TOK, TOK), 0) < lax.broadcasted_iota(jnp.int32, (TOK, TOK), 1)
    )
    before = jnp.dot(
        hits.astype(BF16), jnp.where(earlier, 1.0, 0.0).astype(BF16), preferred_element_type=F32
    )
    meta_low[ex, 0:EXPERTS, :] = jnp.where(hits > 0.5, before, -1.0).astype(BF16)
    meta_low[ex, EXPERTS : 2 * EXPERTS, :] = gates.astype(BF16)

    pl.semaphore_wait(barrier, EXPERTS + 2)

    def m_copy(i, slot, to):
        return remote(meta_low.at[slot], meta_low.at[slot], m_send.at[i], m_recv.at[i], {"expert": to})

    def meta_send(i, carry):
        m_copy(i, ex, lax.rem(ex + i, EXPERTS)).start()
        return carry

    lax.fori_loop(1, EXPERTS, meta_send, 0)

    ym8, yp8 = around_y(-1) * 2 + xh, around_y(1) * 2 + xh
    y2 = around_y(2) * 2 + xh
    flip = 1 - 2 * xh
    lower, upper = pl.ds(0, TOK // 2), pl.ds(TOK // 2, TOK // 2)

    def a_copy(kind, q, src8, rows, to):
        ref = tok.at[src8, q] if rows is None else tok.at[src8, q, rows]
        return remote(ref, ref, a_send.at[kind, q], a_recv.at[kind, q], to)

    def a_out(kind, q):
        return (
            lambda: a_copy(0, q, me8, None, h_mate),
            lambda: a_copy(1, q, me8, None, at_y(1)),
            lambda: a_copy(2, q, me8, None, at_y(-1)),
            lambda: a_copy(3, q, me8 + flip, None, at_y(1)),
            lambda: a_copy(4, q, me8 + flip, None, at_y(-1)),
            lambda: a_copy(5, q, ym8, lower, at_y(1)),
            lambda: a_copy(6, q, yp8, upper, at_y(-1)),
            lambda: a_copy(7, q, ym8 + flip, lower, at_y(1)),
            lambda: a_copy(8, q, yp8 + flip, upper, at_y(-1)),
        )[kind]()

    def a_in(kind, q):
        return (
            lambda: a_copy(0, q, me8 + flip, None, h_mate),
            lambda: a_copy(1, q, ym8, None, at_y(1)),
            lambda: a_copy(2, q, yp8, None, at_y(-1)),
            lambda: a_copy(3, q, ym8 + flip, None, at_y(1)),
            lambda: a_copy(4, q, yp8 + flip, None, at_y(-1)),
            lambda: a_copy(5, q, y2, lower, at_y(1)),
            lambda: a_copy(6, q, y2, upper, at_y(-1)),
            lambda: a_copy(7, q, y2 + flip, lower, at_y(1)),
            lambda: a_copy(8, q, y2 + flip, upper, at_y(-1)),
        )[kind]()

    def a_own(q):
        for kind in (1, 2):
            a_out(kind, q).start()

    half = DZ // 2

    def bz_copy(way, step, to_send):
        sign = 1 if way == 0 else -1
        dist = step - 1 if to_send else step
        ref = wall.at[around_z(-sign * dist), xl]
        if step == 4:
            ref = ref.at[pl.ds(way * half, half)]
        return remote(ref, ref, bz_send.at[way, step - 1], bz_recv.at[way, step - 1], at_z(sign))

    def bx_copy(i, mine):
        ref = wall.at[around_z(i), xl if mine else 1 - xl]
        if i in (1, 7):
            ref = ref.at[pl.ds(half, half)]
        return remote(ref, ref, bx_send.at[i], bx_recv.at[i], x_mate)

    def bn_copy(way, to_send):
        sign = 1 if way == 0 else -1
        ref = wall.at[around_z(0 if to_send else -sign), 1 - xl, pl.ds(0, half)]
        return remote(ref, ref, bn_send.at[way], bn_recv.at[way], at_z(sign))

    for q in range(NQ):
        for j in range(2):
            og_copy(q, j).wait()
        a_out(0, q).start()
        if q < 2:
            a_own(q)
        if q == 0:
            w_copy.wait()
            bz_copy(0, 1, True).start()
            bz_copy(1, 1, True).start()
        if q == 2:
            bx_copy(0, True).start()

    def factors(s, carry):
        row = lax.rem(s, 2) * 8 + s // 2
        for part in range(2):
            lanes = pl.ds(part * (FF // 2), FF // 2)
            g = saved_ref[s, :, part * (FF // 2) : (part + 1) * (FF // 2)].astype(F32)
            u = saved_ref[s, :, FF + part * (FF // 2) : FF + (part + 1) * (FF // 2)].astype(F32)
            sig = jax.nn.sigmoid(g)
            silu = g * sig
            act_low[row, :, lanes] = (silu * u).astype(BF16)
            fac_g[row, :, lanes] = u * sig * (1.0 + g * (1.0 - sig))
            fac_u[row, :, lanes] = silu
        return carry

    saved_copy.wait()
    lax.fori_loop(0, 4, factors, 0)

    def meta_wait(i, carry):
        m_copy(i, lax.rem(ex - i + EXPERTS, EXPERTS), ex).wait_recv()
        return carry

    cap_row = lax.broadcasted_iota(jnp.int32, (CAP, TOK), 0).astype(F32)

    def choose(s, carry):
        hit = cap_row == meta[s, pl.ds(ex, 1), :]
        value = jnp.where(hit, meta[s, pl.ds(EXPERTS + ex, 1), :], 0.0)
        row = lax.rem(s, 2) * 8 + s // 2
        gate[row] = jnp.broadcast_to(jnp.sum(value, axis=1, keepdims=True), (CAP, TOK))
        return carry


    def choose_both(s8, carry):
        s = s8 * 2 + core
        mate_ex = (y * 2 + xh) * 2 + (1 - core)
        mine = cap_row == meta[s, pl.ds(ex, 1), :]
        its = cap_row == meta[s, pl.ds(mate_ex, 1), :]
        sel[s8, 0:CAP, :] = jnp.where(mine, 1.0, 0.0).astype(BF16)
        sel[s8, CAP : 2 * CAP, :] = jnp.where(its, 1.0, 0.0).astype(BF16)
        return carry

    def choose_rows():
        lax.fori_loop(1, EXPERTS, meta_wait, 0)
        meta[...] = meta_low[...].astype(F32)
        lax.fori_loop(0, 16, choose, 0)
        lax.fori_loop(0, 8, choose_both, 0)

    def s_copy(q, mine):
        c = core if mine else 1 - core
        return remote(stage.at[q], routed.at[q, c], s_send.at[q], s_recv.at[q], c_mate)

    def select(q):
        def one(s8, carry):
            got = jnp.dot(sel[s8], tok[s8, q], preferred_element_type=F32).astype(BF16)
            routed[q, core, s8] = got[0:CAP]
            stage[q, s8] = got[CAP : 2 * CAP]
            return carry

        lax.fori_loop(0, 8, one, 0)
        s_copy(q, True).start()

    def partial_sum(q, j):
        rows = routed[q, :, :, :, j * DZ : (j + 1) * DZ].reshape(16 * CAP, DZ).astype(F32)
        scale = gate[...].reshape(16 * CAP, TOK)[:, 0:1]
        weighted = (rows * scale).astype(BF16)
        part[j] = lax.dot_general(
            weighted,
            act_low[...].reshape(16 * CAP, FF),
            (((0,), (0,)), ((), ())),
            preferred_element_type=F32,
        )

    def c_half(way, order):
        return remote(
            rs_half.at[way, order],
            rs_half_in.at[way, order],
            c_send.at[way, 0, order],
            c_recv.at[way, 0, order],
            at_z(1 - 2 * way),
        )

    def c_full(way, hop, order):
        return remote(
            rs_out.at[way, hop - 1, order],
            rs_in.at[way, hop - 1, order],
            c_send.at[way, hop, order],
            c_recv.at[way, hop, order],
            at_z(1 - 2 * way),
        )

    def reduce(q):
        for j in range(2):
            partial_sum(q, j)
            if q == 0:
                for way in range(2):
                    rs_half[way, j] = part[j, way * half : (way + 1) * half, :].astype(BF16)
                    c_half(way, j).start()

    def chain(q):
        order, hop = (q - 1) % 2, (q + 1) // 2
        for way in range(2):
            if hop == 1:
                c_half(way, order).wait_recv()
                mid = slice(way * half, (way + 1) * half)
                rest = slice((1 - way) * half, (2 - way) * half)
                rs_out[way, 0, order, mid] = (
                    part[way, mid, :] + rs_half_in[way, order].astype(F32)
                ).astype(BF16)
                rs_out[way, 0, order, rest] = part[way, rest, :].astype(BF16)
            else:
                c_full(way, hop - 1, order).wait_recv()
                rs_out[way, hop - 1, order] = (
                    part[way] + rs_in[way, hop - 2, order].astype(F32)
                ).astype(BF16)
            c_full(way, hop, order).start()

    def f_copy():
        return remote(fin_out, fin_in, f_send, f_recv, x_mate)

    def back(q):
        for c in range(2):
            rows = slice(c * 8 * CAP, (c + 1) * 8 * CAP)
            got = acc[rows, :]
            for j in range(2):
                dist, order = PIECES[q][j]
                got = got + jnp.dot(
                    routed[q, c, :, :, j * DZ : (j + 1) * DZ].reshape(8 * CAP, DZ),
                    wall[around_z(dist), column(order)],
                    preferred_element_type=F32,
                )
            acc[rows, :] = got

    acc[...] = jnp.zeros_like(acc)

    for t in range(NQ + 2):
        if t < NQ:
            a_in(0, t).wait_recv()
            a_out(3, t).start()
            a_out(4, t).start()
            a_in(1, t).wait_recv()
            a_out(5, t).start()
            a_in(2, t).wait_recv()
            a_out(6, t).start()
        for q in {0: (2,), 1: (3, 4)}.get(t, (t + 3,)):
            if q < NQ:
                a_own(q)
        if 0 <= t - 1 < NQ:
            a_in(3, t - 1).wait_recv()
            a_out(7, t - 1).start()
            a_in(4, t - 1).wait_recv()
            a_out(8, t - 1).start()
        if t in (1, 2, 3):
            for way in range(2):
                bz_copy(way, t, False).wait_recv()
                bz_copy(way, t + 1, True).start()
        if t == 2:
            bx_copy(0, False).wait_recv()
            bn_copy(0, True).start()
            bn_copy(1, True).start()
        if t == 5:
            bz_copy(0, 4, False).wait_recv()
            bz_copy(1, 4, False).wait_recv()
        for i in {1: (1, 7), 2: (2, 6), 3: (3, 5), 5: (4,)}.get(t, ()):
            bx_copy(i, True).start()
        if t < 2:
            lax.fori_loop(4 + 6 * t, 10 + 6 * t, factors, 0)
        if t == 1:
            choose_rows()
        if t == 7:
            for i in (1, 7, 2, 6):
                bx_copy(i, False).wait_recv()
            bn_copy(0, False).wait_recv()
            bn_copy(1, False).wait_recv()
        if 0 <= t - 2 < NQ:
            for kind in (5, 6, 7, 8):
                a_in(kind, t - 2).wait_recv()
            select(t - 2)
            if t - 3 >= 1:
                chain(t - 3)
            if t == 7:
                back(3)
            if t == 8:
                back(4)
                back(5)
            s_copy(t - 2, False).wait_recv()
            reduce(t - 2)

    def g_copy(i, src, dst, to):
        return remote(sc_out.at[src], sc_in.at[dst], g_send.at[i], g_recv.at[i], {"expert": to})

    def finish(c):
        def one(s8, carry):
            s = s8 * 2 + c
            row = c * 8 + s8
            out = acc[pl.ds(pl.multiple_of(row * CAP, CAP), CAP), :]
            scale = gate[row][:, 0:1]
            grad = out * scale
            silu = fac_u[row]
            u = saved_ref[s, :, FF : 2 * FF].astype(F32)
            pre_ref[s, :, 0:FF] = (grad * fac_g[row]).astype(BF16)
            pre_ref[s, :, FF : 2 * FF] = (grad * silu).astype(BF16)
            score = jnp.sum(out * (silu * u), axis=1, keepdims=True)
            sc_out[s] = jnp.broadcast_to(score, (CAP, TOK))
            return carry

        lax.fori_loop(0, 8, one, 0)

    def last(order):
        c_full(0, 3, order).wait_recv()
        c_full(1, 3, order).wait_recv()
        return part[order] + rs_in[0, 2, order].astype(F32) + rs_in[1, 2, order].astype(F32)

    back(6)
    back(7)
    fin_out[...] = last(0).astype(BF16)
    f_copy().start()
    bx_copy(3, False).wait_recv()
    bx_copy(5, False).wait_recv()
    back(1)
    back(2)
    bx_copy(4, False).wait_recv()
    back(0)

    def pre_copy(c, s8):
        ref = s8 * 2 + c
        return pltpu.make_async_copy(pre_ref.at[ref], pre_hbm.at[ref], pre_sem.at[ref])

    def pre_out(c):
        for s8 in range(8):
            pre_copy(c, s8).start()

    finish(0)
    pre_out(0)
    finish(1)
    pre_out(1)

    def score_send(i, carry):
        to = lax.rem(ex + i, EXPERTS)
        g_copy(i, to, ex, to).start()
        return carry

    lax.fori_loop(1, EXPERTS, score_send, 0)
    sc_in[ex] = sc_out[ex]

    own = last(1)
    f_copy().wait_recv()
    down_ref[...] = (own + fin_in[...].astype(F32)).astype(BF16)

    def score_wait(i, carry):
        g_copy(i, ex, lax.rem(ex - i + EXPERTS, EXPERTS), ex).wait_recv()
        return carry

    lax.fori_loop(1, EXPERTS, score_wait, 0)

    rows = [jnp.zeros((1, TOK), F32) for _ in range(4)]
    for e in range(EXPERTS):
        hit = cap_row == meta[ex, e : e + 1, :]
        value = jnp.sum(jnp.where(hit, sc_in[e], 0.0), axis=0, keepdims=True)
        for k in range(4):
            rows[k] = rows[k] + jnp.where(ids_ref[k : k + 1, :] == float(e), value, 0.0)
    for k in range(4):
        gate_ref[k : k + 1, :] = rows[k]
        gate_ref[4 + k : 5 + k, :] = rows[k]

    def drain_peers(i, carry):
        to = lax.rem(ex + i, EXPERTS)
        m_copy(i, ex, to).wait_send()
        g_copy(i, to, ex, to).wait_send()
        return carry

    lax.fori_loop(1, EXPERTS, drain_peers, 0)
    for q in range(NQ):
        for kind in range(9):
            a_out(kind, q).wait_send()
        s_copy(q, True).wait_send()
        bx_copy(q, True).wait_send()
        for c in range(2):
            pre_copy(c, q).wait()
    for way in range(2):
        for step in range(1, 5):
            bz_copy(way, step, True).wait_send()
        bn_copy(way, True).wait_send()
        for order in range(2):
            c_half(way, order).wait_send()
            for hop in range(1, 4):
                c_full(way, hop, order).wait_send()
    f_copy().wait_send()


def shards(out_grad, expert_ids, gate_weights, saved_acts, down_weight):
    small = jnp.concatenate([expert_ids.astype(F32), gate_weights.astype(F32)], axis=1).T
    vmem = pl.BlockSpec(memory_space=pltpu.VMEM)
    hbm = pl.BlockSpec(memory_space=pl.ANY)
    dma = pltpu.SemaphoreType.DMA
    pre, down, gate_t = pl.pallas_call(
        kernel,
        out_shape=(
            jax.ShapeDtypeStruct((EXPERTS, CAP, 2 * FF), BF16),
            jax.ShapeDtypeStruct((DZ, FF), BF16),
            jax.ShapeDtypeStruct((8, TOK), F32),
        ),
        in_specs=[hbm, vmem, hbm, hbm],
        out_specs=(hbm, vmem, vmem),
        scratch_shapes=[
            pltpu.VMEM((EXPERTS, CAP, 2 * FF), BF16),
            pltpu.VMEM((EXPERTS, CAP, 2 * FF), BF16),
            pltpu.VMEM((8, NQ, TOK, 2 * DZ), BF16),
            pltpu.VMEM((NQ, 2, 8, CAP, 2 * DZ), BF16),
            pltpu.VMEM((NQ, 8, CAP, 2 * DZ), BF16),
            pltpu.VMEM((8, 2 * CAP, TOK), BF16),
            pltpu.VMEM((16, CAP, TOK), F32),
            pltpu.VMEM((16, 2 * EXPERTS, TOK), BF16),
            pltpu.VMEM((16, 2 * EXPERTS, TOK), F32),
            pltpu.VMEM((NZ, 2, DZ, FF), BF16),
            pltpu.VMEM((16, CAP, FF), BF16),
            pltpu.VMEM((16, CAP, FF), F32),
            pltpu.VMEM((16, CAP, FF), F32),
            pltpu.VMEM((16 * CAP, FF), F32),
            pltpu.VMEM((2, 2, DZ // 2, FF), BF16),
            pltpu.VMEM((2, 3, 2, DZ, FF), BF16),
            pltpu.VMEM((2, 2, DZ // 2, FF), BF16),
            pltpu.VMEM((2, 3, 2, DZ, FF), BF16),
            pltpu.VMEM((DZ, FF), BF16),
            pltpu.VMEM((DZ, FF), BF16),
            pltpu.VMEM((2, DZ, FF), F32),
            pltpu.VMEM((16, CAP, TOK), F32),
            pltpu.VMEM((16, CAP, TOK), F32),
            dma((9, NQ)), dma((9, NQ)),
            dma((NQ,)), dma((NQ,)),
            dma((EXPERTS,)), dma((EXPERTS,)),
            dma((2, 4)), dma((2, 4)),
            dma((NZ,)), dma((NZ,)),
            dma((2,)), dma((2,)),
            dma((2, 4, 2)), dma((2, 4, 2)),
            dma(()), dma(()),
            dma((EXPERTS,)), dma((EXPERTS,)),
            dma((NQ, 2)), dma(()), dma(()), dma((EXPERTS,)),
        ],
        compiler_params=pltpu.CompilerParams(
            collective_id=0, has_side_effects=True, vmem_limit_bytes=60 * 1024 * 1024
        ),
    )(out_grad, small, saved_acts[0, :, 0], down_weight[0])
    return pre[None, :, None], down[None], gate_t[:4].T


def solution(mesh):
    placed = (
        P(("dp", "expert"), None),
        P(("dp", "expert"), None),
        P(("dp", "expert"), None),
        P("dp", None, "expert", None, None),
        P("expert", "dp", None),
    )
    return jax.shard_map(
        shards,
        mesh=mesh,
        in_specs=placed,
        out_specs=(
            P("dp", None, "expert", None, None),
            P("expert", "dp", None),
            P(("dp", "expert"), None),
        ),
        check_vma=False,
    )
```

time: 159 us -> 129 us (0.81)
  Pallas kernels: 151 us -> 121 us
    pallas_call x1, Pallas kernels: 151 us -> 121 us  [shards(): pl.pallas_call(kernel, out_shape=(jax.ShapeDtypeStruct((EXPERTS, CAP, 2 *...]
where the time goes in v2:
time: 129 us
  Pallas kernels  121 us (94%)
  local copies, waits for them, and re-layouts  5.29 us (4%)
  other arithmetic  1.97 us (2%)
    pallas_call x1, Pallas kernels, shards(): pl.pallas_call(kernel, out_shape=(jax.ShapeDtypeStruct((EXPERTS, CAP, 2 *...  121 us
    unnamed x4, local copies, waits for them, and re-layouts  4.03 us

profile of v2, /device:TPU:1, one launch (start us, length us, event | category | flops | bytes accessed | tf_op | source)
XLA Modules:
  0.0 128.8 jit_solution(14130812593282514749)
XLA Ops:
  0.6 0.7 convert_element_type.6
  1.3 0.7 convert_element_type.7
  2.0 0.6 maximum_bitcast_fusion.ids_ref
  2.6 120.9 %shard_map.76 = (bf16[16,48,1536]{2,1,0:T(8,128)(2,1)}, bf16[256,768]{1,0:T(8,128)(2,1)}, f32[8,128]{1,0:T(8,128)}) custom-call(bf16[128,4096]{1,0:T(8,128)(2,1)} %og_ref.1, f32[8,128]{1,0:T(8,128)} %maximum_bitcast_fusion.ids_ref, bf16[16,48,1536]{2,1,0:T(8,128)(2,1)} %bitcast.10, bf16[256,768]{1,0:T(8,128)(2,1)} %bitcast.12), custom_call_target="tpu_custom_call" | custom-call | tf_op jit(solution)/shard_map/pallas_call | solution.py:491
  123.5 1.3 slice_bitcast_fusion
  124.7 0.0 copy-start
  124.7 3.3 %copy.11 = bf16[1,16,1,48,1536]{4,3,2,1,0:T(8,128)(2,1)} copy(bf16[1,16,1,48,1536]{4,3,2,1,0:T(8,128)(2,1)} %bitcast.11) | data formatting | bytes 4718592
  128.0 0.0 copy-done
  128.0 0.7 copy.12
Async XLA Ops:
  124.7 3.3 %copy-start = (bf16[256,768]{1,0:T(8,128)(2,1)S(1)}, bf16[256,768]{1,0:T(8,128)(2,1)}, u32[]{:S(2)}) copy-start(bf16[256,768]{1,0:T(8,128)(2,1)} %get-tuple-element.7) | copy-start | bytes 1179652

commit v3 on v2

--- a/solution.py
+++ b/solution.py
@@ -30,7 +30,7 @@
 
 
 def kernel(
-    og_ref, ids_ref, saved_hbm, w_ref,
+    og_ref, ids_ref, weights_ref, saved_hbm, w_ref,
     pre_hbm, down_ref, gate_ref,
     saved_ref, pre_ref, tok, routed, stage, sel, gate, meta_low, meta, wall, act_low, fac_g, fac_u, acc,
     rs_half, rs_out, rs_half_in, rs_in, fin_out, fin_in, part, sc_out, sc_in,
@@ -96,13 +96,14 @@
         if q == 1:
             w_copy.start()
     saved_copy.start()
-    expert_row = lax.broadcasted_iota(jnp.int32, (EXPERTS, TOK), 0).astype(F32)
+    expert_row = lax.broadcasted_iota(jnp.int32, (EXPERTS, TOK), 0)
+    weight_rows = weights_ref[...].astype(F32)
     hits = jnp.zeros((EXPERTS, TOK), F32)
     gates = jnp.zeros((EXPERTS, TOK), F32)
     for k in range(4):
         eq = expert_row == ids_ref[k : k + 1, :]
         hits = hits + jnp.where(eq, 1.0, 0.0)
-        gates = gates + jnp.where(eq, ids_ref[4 + k : 5 + k, :], 0.0)
+        gates = gates + jnp.where(eq, weight_rows[k : k + 1, :], 0.0)
     earlier = (
         lax.broadcasted_iota(jnp.int32, (TOK, TOK), 0) < lax.broadcasted_iota(jnp.int32, (TOK, TOK), 1)
     )
@@ -114,14 +115,6 @@
 
     pl.semaphore_wait(barrier, EXPERTS + 2)
 
-    def m_copy(i, slot, to):
-        return remote(meta_low.at[slot], meta_low.at[slot], m_send.at[i], m_recv.at[i], {"expert": to})
-
-    def meta_send(i, carry):
-        m_copy(i, ex, lax.rem(ex + i, EXPERTS)).start()
-        return carry
-
-    lax.fori_loop(1, EXPERTS, meta_send, 0)
 
     ym8, yp8 = around_y(-1) * 2 + xh, around_y(1) * 2 + xh
     y2 = around_y(2) * 2 + xh
@@ -164,13 +157,18 @@
 
     half = DZ // 2
 
-    def bz_copy(way, step, to_send):
+    def bz_copy(way, step, h, to_send):
         sign = 1 if way == 0 else -1
         dist = step - 1 if to_send else step
-        ref = wall.at[around_z(-sign * dist), xl]
-        if step == 4:
-            ref = ref.at[pl.ds(way * half, half)]
-        return remote(ref, ref, bz_send.at[way, step - 1], bz_recv.at[way, step - 1], at_z(sign))
+        ref = wall.at[around_z(-sign * dist), xl, pl.ds(h * half, half)]
+        sems = (way, step - 1, h)
+        return remote(ref, ref, bz_send.at[sems], bz_recv.at[sems], at_z(sign))
+
+    def bz_next(step, h, ways=(0, 1)):
+        for way in ways:
+            bz_copy(way, step, h, False).wait_recv()
+            if step < 3 or (step == 3 and h == way):
+                bz_copy(way, step + 1, h, True).start()
 
     def bx_copy(i, mine):
         ref = wall.at[around_z(i), xl if mine else 1 - xl]
@@ -182,6 +180,20 @@
         sign = 1 if way == 0 else -1
         ref = wall.at[around_z(0 if to_send else -sign), 1 - xl, pl.ds(0, half)]
         return remote(ref, ref, bn_send.at[way], bn_recv.at[way], at_z(sign))
+
+    w_copy.wait()
+    for h in range(2):
+        for way in range(2):
+            bz_copy(way, 1, h, True).start()
+
+    def m_copy(i, slot, to):
+        return remote(meta_low.at[slot], meta_low.at[slot], m_send.at[i], m_recv.at[i], {"expert": to})
+
+    def meta_send(i, carry):
+        m_copy(i, ex, lax.rem(ex + i, EXPERTS)).start()
+        return carry
+
+    lax.fori_loop(1, EXPERTS, meta_send, 0)
 
     for q in range(NQ):
         for j in range(2):
@@ -189,10 +201,6 @@
         a_out(0, q).start()
         if q < 2:
             a_own(q)
-        if q == 0:
-            w_copy.wait()
-            bz_copy(0, 1, True).start()
-            bz_copy(1, 1, True).start()
         if q == 2:
             bx_copy(0, True).start()
 
@@ -329,6 +337,8 @@
     acc[...] = jnp.zeros_like(acc)
 
     for t in range(NQ + 2):
+        if 1 <= t - 3 < NQ - 1:
+            chain(t - 3)
         if t < NQ:
             a_in(0, t).wait_recv()
             a_out(3, t).start()
@@ -337,7 +347,7 @@
             a_out(5, t).start()
             a_in(2, t).wait_recv()
             a_out(6, t).start()
-        for q in {0: (2,), 1: (3, 4)}.get(t, (t + 3,)):
+        for q in (t + 2,):
             if q < NQ:
                 a_own(q)
         if 0 <= t - 1 < NQ:
@@ -345,18 +355,23 @@
             a_out(7, t - 1).start()
             a_in(4, t - 1).wait_recv()
             a_out(8, t - 1).start()
-        if t in (1, 2, 3):
-            for way in range(2):
-                bz_copy(way, t, False).wait_recv()
-                bz_copy(way, t + 1, True).start()
+        if t == 0:
+            bz_next(1, 0)
+        if t == 1:
+            bz_next(1, 1)
         if t == 2:
+            bz_next(2, 0)
             bx_copy(0, False).wait_recv()
             bn_copy(0, True).start()
             bn_copy(1, True).start()
-        if t == 5:
-            bz_copy(0, 4, False).wait_recv()
-            bz_copy(1, 4, False).wait_recv()
-        for i in {1: (1, 7), 2: (2, 6), 3: (3, 5), 5: (4,)}.get(t, ()):
+        if t == 3:
+            bz_next(3, 0)
+        if t == 4:
+            bz_next(3, 1)
+        if t == 6:
+            bz_copy(0, 4, 0, False).wait_recv()
+            bz_copy(1, 4, 1, False).wait_recv()
+        for i in {1: (1, 7), 4: (3, 5), 6: (4,)}.get(t, ()):
             bx_copy(i, True).start()
         if t < 2:
             lax.fori_loop(4 + 6 * t, 10 + 6 * t, factors, 0)
@@ -371,8 +386,10 @@
             for kind in (5, 6, 7, 8):
                 a_in(kind, t - 2).wait_recv()
             select(t - 2)
-            if t - 3 >= 1:
-                chain(t - 3)
+            if t == 2:
+                bz_next(2, 1)
+                bx_copy(2, True).start()
+                bx_copy(6, True).start()
             if t == 7:
                 back(3)
             if t == 8:
@@ -408,12 +425,33 @@
 
     back(6)
     back(7)
-    fin_out[...] = last(0).astype(BF16)
-    f_copy().start()
     bx_copy(3, False).wait_recv()
     bx_copy(5, False).wait_recv()
     back(1)
     back(2)
+    def drain_meta(i, carry):
+        m_copy(i, ex, lax.rem(ex + i, EXPERTS)).wait_send()
+        return carry
+
+    lax.fori_loop(1, EXPERTS, drain_meta, 0)
+    for q in range(NQ):
+        for kind in range(9):
+            a_out(kind, q).wait_send()
+        s_copy(q, True).wait_send()
+        bx_copy(q, True).wait_send()
+    for way in range(2):
+        for step in range(1, 5):
+            for h in range(2):
+                if step < 4 or h == way:
+                    bz_copy(way, step, h, True).wait_send()
+        bn_copy(way, True).wait_send()
+        for order in range(2):
+            c_half(way, order).wait_send()
+            for hop in range(1, 4):
+                if hop < 3:
+                    c_full(way, hop, order).wait_send()
+    fin_out[...] = last(0).astype(BF16)
+    f_copy().start()
     bx_copy(4, False).wait_recv()
     back(0)
 
@@ -453,38 +491,26 @@
         hit = cap_row == meta[ex, e : e + 1, :]
         value = jnp.sum(jnp.where(hit, sc_in[e], 0.0), axis=0, keepdims=True)
         for k in range(4):
-            rows[k] = rows[k] + jnp.where(ids_ref[k : k + 1, :] == float(e), value, 0.0)
+            rows[k] = rows[k] + jnp.where(ids_ref[k : k + 1, :] == e, value, 0.0)
     for k in range(4):
         gate_ref[k : k + 1, :] = rows[k]
-        gate_ref[4 + k : 5 + k, :] = rows[k]
-
-    def drain_peers(i, carry):
+
+    def drain_scores(i, carry):
         to = lax.rem(ex + i, EXPERTS)
-        m_copy(i, ex, to).wait_send()
         g_copy(i, to, ex, to).wait_send()
         return carry
 
-    lax.fori_loop(1, EXPERTS, drain_peers, 0)
+    lax.fori_loop(1, EXPERTS, drain_scores, 0)
+    f_copy().wait_send()
+    for way in range(2):
+        for order in range(2):
+            c_full(way, 3, order).wait_send()
     for q in range(NQ):
-        for kind in range(9):
-            a_out(kind, q).wait_send()
-        s_copy(q, True).wait_send()
-        bx_copy(q, True).wait_send()
         for c in range(2):
             pre_copy(c, q).wait()
-    for way in range(2):
-        for step in range(1, 5):
-            bz_copy(way, step, True).wait_send()
-        bn_copy(way, True).wait_send()
-        for order in range(2):
-            c_half(way, order).wait_send()
-            for hop in range(1, 4):
-                c_full(way, hop, order).wait_send()
-    f_copy().wait_send()
 
 
 def shards(out_grad, expert_ids, gate_weights, saved_acts, down_weight):
-    small = jnp.concatenate([expert_ids.astype(F32), gate_weights.astype(F32)], axis=1).T
     vmem = pl.BlockSpec(memory_space=pltpu.VMEM)
     hbm = pl.BlockSpec(memory_space=pl.ANY)
     dma = pltpu.SemaphoreType.DMA
@@ -493,9 +519,9 @@
         out_shape=(
             jax.ShapeDtypeStruct((EXPERTS, CAP, 2 * FF), BF16),
             jax.ShapeDtypeStruct((DZ, FF), BF16),
-            jax.ShapeDtypeStruct((8, TOK), F32),
+            jax.ShapeDtypeStruct((4, TOK), F32),
         ),
-        in_specs=[hbm, vmem, hbm, hbm],
+        in_specs=[hbm, vmem, vmem, hbm, hbm],
         out_specs=(hbm, vmem, vmem),
         scratch_shapes=[
             pltpu.VMEM((EXPERTS, CAP, 2 * FF), BF16),
@@ -524,7 +550,7 @@
             dma((9, NQ)), dma((9, NQ)),
             dma((NQ,)), dma((NQ,)),
             dma((EXPERTS,)), dma((EXPERTS,)),
-            dma((2, 4)), dma((2, 4)),
+            dma((2, 4, 2)), dma((2, 4, 2)),
             dma((NZ,)), dma((NZ,)),
             dma((2,)), dma((2,)),
             dma((2, 4, 2)), dma((2, 4, 2)),
@@ -535,8 +561,8 @@
         compiler_params=pltpu.CompilerParams(
             collective_id=0, has_side_effects=True, vmem_limit_bytes=60 * 1024 * 1024
         ),
-    )(out_grad, small, saved_acts[0, :, 0], down_weight[0])
-    return pre[None, :, None], down[None], gate_t[:4].T
+    )(out_grad, expert_ids.T, gate_weights.T, saved_acts[0, :, 0], down_weight[0])
+    return pre[None, :, None], down[None], gate_t.T
 
 
 def solution(mesh):

time: 129 us -> 124 us (0.961)
  Pallas kernels: 121 us -> 118 us
  other arithmetic: 1.97 us -> 0 us
    pallas_call x1, Pallas kernels: 121 us -> 118 us  [shards(): pl.pallas_call(kernel, out_shape=(jax.ShapeDtypeStruct((EXPERTS, CAP, 2 *...]
    convert_element_type x2 -> x0, other arithmetic: 1.37 us -> none  [the longest x1 0.68 us: shards(): expert_ids.astype(F32)]
    unnamed x4 -> x7, local copies, waits for them, and re-layouts: 4.03 us -> 4.61 us
where the time goes in v3:
time: 124 us
  Pallas kernels  118 us (95%)
  local copies, waits for them, and re-layouts  4.61 us (4%)
    pallas_call x1, Pallas kernels, shards(): pl.pallas_call(kernel, out_shape=(jax.ShapeDtypeStruct((EXPERTS, CAP, 2 *...  118 us
    unnamed x7, local copies, waits for them, and re-layouts  4.61 us

profile of v3, /device:TPU:1, one launch (start us, length us, event | category | flops | bytes accessed | tf_op | source)
XLA Modules:
  0.0 123.7 jit_solution(3526729703754347521)
XLA Ops:
  0.6 118.5 %shard_map.76 = (bf16[16,48,1536]{2,1,0:T(8,128)(2,1)}, bf16[256,768]{1,0:T(8,128)(2,1)}, f32[4,128]{1,0:T(4,128)}) custom-call(bf16[128,4096]{1,0:T(8,128)(2,1)} %og_ref.1, s32[4,128]{1,0:T(4,128)} %bitcast.13, bf16[4,128]{1,0:T(4,128)(2,1)} %bitcast.15, bf16[16,48,1536]{2,1,0:T(8,128)(2,1)} %bitcast.10, bf16[256,768]{1,0:T(8,128)(2,1)} %bitcast.11), custom_call_target="tpu_custom_call" | custom-call | tf_op jit(solution)/shard_map/pallas_call | solution.py:517
  119.1 0.0 copy-start
  119.1 0.0 copy-start.1
  119.1 3.3 %copy.12 = bf16[1,16,1,48,1536]{4,3,2,1,0:T(8,128)(2,1)} copy(bf16[1,16,1,48,1536]{4,3,2,1,0:T(8,128)(2,1)} %bitcast.9) | data formatting | bytes 4718592
  122.4 0.0 copy-done
  122.4 0.7 copy.13
  123.2 0.0 copy-done.1
  123.2 0.6 copy.14
Async XLA Ops:
  119.1 3.3 %copy-start = (bf16[256,768]{1,0:T(8,128)(2,1)S(1)}, bf16[256,768]{1,0:T(8,128)(2,1)}, u32[]{:S(2)}) copy-start(bf16[256,768]{1,0:T(8,128)(2,1)} %get-tuple-element.7) | copy-start | bytes 1179652
  119.1 4.0 %copy-start.1 = (f32[4,128]{1,0:T(4,128)S(1)}, f32[4,128]{1,0:T(4,128)}, u32[]{:S(2)}) copy-start(f32[4,128]{1,0:T(4,128)} %get-tuple-element.8) | copy-start | bytes 6148

commit v4 on v3

--- a/solution.py
+++ b/solution.py
@@ -35,7 +35,7 @@
     saved_ref, pre_ref, tok, routed, stage, sel, gate, meta_low, meta, wall, act_low, fac_g, fac_u, acc,
     rs_half, rs_out, rs_half_in, rs_in, fin_out, fin_in, part, sc_out, sc_in,
     a_send, a_recv, s_send, s_recv, m_send, m_recv,
-    bz_send, bz_recv, bx_send, bx_recv, bn_send, bn_recv, c_send, c_recv, f_send, f_recv,
+    bz_send, bz_recv, bx_send, bx_recv, bn_send, bn_recv, c_send, c_recv, l_send, l_recv, f_send, f_recv,
     g_send, g_recv, og_sem, w_sem, saved_sem, pre_sem,
 ):
     dp = lax.axis_index("dp")
@@ -292,6 +292,16 @@
             at_z(1 - 2 * way),
         )
 
+    def c_last(way, h):
+        rows = pl.ds(h * half, half)
+        return remote(
+            rs_out.at[way, 2, 0, rows],
+            rs_in.at[way, 2, 0, rows],
+            l_send.at[way, h],
+            l_recv.at[way, h],
+            at_z(1 - 2 * way),
+        )
+
     def reduce(q):
         for j in range(2):
             partial_sum(q, j)
@@ -316,10 +326,15 @@
                 rs_out[way, hop - 1, order] = (
                     part[way] + rs_in[way, hop - 2, order].astype(F32)
                 ).astype(BF16)
-            c_full(way, hop, order).start()
-
-    def f_copy():
-        return remote(fin_out, fin_in, f_send, f_recv, x_mate)
+            if (hop, order) == (3, 0):
+                c_last(way, 0).start()
+                c_last(way, 1).start()
+            else:
+                c_full(way, hop, order).start()
+
+    def f_copy(h):
+        rows = pl.ds(h * half, half)
+        return remote(fin_out.at[rows], fin_in.at[rows], f_send.at[h], f_recv.at[h], x_mate)
 
     def back(q):
         for c in range(2):
@@ -418,10 +433,12 @@
 
         lax.fori_loop(0, 8, one, 0)
 
-    def last(order):
-        c_full(0, 3, order).wait_recv()
-        c_full(1, 3, order).wait_recv()
-        return part[order] + rs_in[0, 2, order].astype(F32) + rs_in[1, 2, order].astype(F32)
+    def last(order, rows):
+        return (
+            part[order, rows, :]
+            + rs_in[0, 2, order, rows].astype(F32)
+            + rs_in[1, 2, order, rows].astype(F32)
+        )
 
     back(6)
     back(7)
@@ -450,8 +467,12 @@
             for hop in range(1, 4):
                 if hop < 3:
                     c_full(way, hop, order).wait_send()
-    fin_out[...] = last(0).astype(BF16)
-    f_copy().start()
+    for h in range(2):
+        c_last(0, h).wait_recv()
+        c_last(1, h).wait_recv()
+        rows = slice(h * half, (h + 1) * half)
+        fin_out[rows, :] = last(0, rows).astype(BF16)
+        f_copy(h).start()
     bx_copy(4, False).wait_recv()
     back(0)
 
@@ -476,9 +497,12 @@
     lax.fori_loop(1, EXPERTS, score_send, 0)
     sc_in[ex] = sc_out[ex]
 
-    own = last(1)
-    f_copy().wait_recv()
-    down_ref[...] = (own + fin_in[...].astype(F32)).astype(BF16)
+    c_full(0, 3, 1).wait_recv()
+    c_full(1, 3, 1).wait_recv()
+    for h in range(2):
+        f_copy(h).wait_recv()
+        rows = slice(h * half, (h + 1) * half)
+        down_ref[rows, :] = (last(1, rows) + fin_in[rows, :].astype(F32)).astype(BF16)
 
     def score_wait(i, carry):
         g_copy(i, ex, lax.rem(ex - i + EXPERTS, EXPERTS), ex).wait_recv()
@@ -501,10 +525,12 @@
         return carry
 
     lax.fori_loop(1, EXPERTS, drain_scores, 0)
-    f_copy().wait_send()
+    f_copy(0).wait_send()
+    f_copy(1).wait_send()
     for way in range(2):
-        for order in range(2):
-            c_full(way, 3, order).wait_send()
+        c_full(way, 3, 1).wait_send()
+        c_last(way, 0).wait_send()
+        c_last(way, 1).wait_send()
     for q in range(NQ):
         for c in range(2):
             pre_copy(c, q).wait()
@@ -554,7 +580,8 @@
             dma((NZ,)), dma((NZ,)),
             dma((2,)), dma((2,)),
             dma((2, 4, 2)), dma((2, 4, 2)),
-            dma(()), dma(()),
+            dma((2, 2)), dma((2, 2)),
+            dma((2,)), dma((2,)),
             dma((EXPERTS,)), dma((EXPERTS,)),
             dma((NQ, 2)), dma(()), dma(()), dma((EXPERTS,)),
         ],

time: 124 us -> 123 us (level)
  no operation moved by 1% of the time
where the time goes in v4:
time: 123 us
  Pallas kernels  117 us (95%)
  local copies, waits for them, and re-layouts  4.61 us (4%)
    pallas_call x1, Pallas kernels, shards(): pl.pallas_call(kernel, out_shape=(jax.ShapeDtypeStruct((EXPERTS, CAP, 2 *...  117 us
    unnamed x7, local copies, waits for them, and re-layouts  4.61 us

profile of v4, /device:TPU:1, one launch (start us, length us, event | category | flops | bytes accessed | tf_op | source)
XLA Modules:
  0.0 122.8 jit_solution(6119416196336521488)
XLA Ops:
  0.6 117.5 %shard_map.76 = (bf16[16,48,1536]{2,1,0:T(8,128)(2,1)}, bf16[256,768]{1,0:T(8,128)(2,1)}, f32[4,128]{1,0:T(4,128)}) custom-call(bf16[128,4096]{1,0:T(8,128)(2,1)} %og_ref.1, s32[4,128]{1,0:T(4,128)} %bitcast.13, bf16[4,128]{1,0:T(4,128)(2,1)} %bitcast.15, bf16[16,48,1536]{2,1,0:T(8,128)(2,1)} %bitcast.10, bf16[256,768]{1,0:T(8,128)(2,1)} %bitcast.11), custom_call_target="tpu_custom_call" | custom-call | tf_op jit(solution)/shard_map/pallas_call | solution.py:543
  118.1 0.0 copy-start
  118.1 0.0 copy-start.1
  118.2 3.3 %copy.12 = bf16[1,16,1,48,1536]{4,3,2,1,0:T(8,128)(2,1)} copy(bf16[1,16,1,48,1536]{4,3,2,1,0:T(8,128)(2,1)} %bitcast.9) | data formatting | bytes 4718592
  121.4 0.0 copy-done
  121.4 0.7 copy.13
  122.2 0.0 copy-done.1
  122.2 0.6 copy.14
Async XLA Ops:
  118.1 3.3 %copy-start = (bf16[256,768]{1,0:T(8,128)(2,1)S(1)}, bf16[256,768]{1,0:T(8,128)(2,1)}, u32[]{:S(2)}) copy-start(bf16[256,768]{1,0:T(8,128)(2,1)} %get-tuple-element.7) | copy-start | bytes 1179652
  118.1 4.0 %copy-start.1 = (f32[4,128]{1,0:T(4,128)S(1)}, f32[4,128]{1,0:T(4,128)}, u32[]{:S(2)}) copy-start(f32[4,128]{1,0:T(4,128)} %get-tuple-element.8) | copy-start | bytes 6148
